TPU v7x, 128 devices: a whole 4x4x4 slice. The times are simulated.
128 devices in a mesh: leaf: 64 (over z, y, x), front: 2 (over core).
Axes of the slice: x: 4, y: 4, z: 4, core: 2. Of those that a mesh axis runs over, the one named last changes fastest.
Arguments:
- leaf_rhs: float32 [2, 32, 64, 2, 256], P(None, None, 'leaf', 'front'), may hold values from -6 to 6
- front_rhs: float32 [2, 32, 64, 1024], P(None, None, 'leaf', 'front'), may hold values from -6 to 6
- leaf_inverse: float32 [64, 2, 256, 256], P('leaf', 'front'), may hold values from -2 to 2, as said below
- coupling: float32 [64, 2, 384, 256], P('leaf', 'front'), may hold values from -0.375 to 0.375
- front_factor: float32 [64, 1024, 1024], P('leaf', 'front'), may hold values from -0.1875 to 0.1875
- front_inverse: float32 [64, 1024, 512], P('leaf', 'front'), may hold values from -2 to 2, as said below
- parent: int32 [64, 2], P('leaf', 'front'), may hold values from 0 to 63
- rows: int32 [64, 2, 384], P('leaf', 'front'), may hold values from 0 to 511, as said below
Outputs:
- leaf_solution: float32 [2, 32, 64, 2, 256], P(None, None, 'leaf', 'front')
- front_solution: float32 [2, 32, 64, 1024], P(None, None, 'leaf', 'front')
Inputs may be any that keep to these rules, and one draw needn't show every extreme that they name: `rows`: the 384 row indices of one child are distinct. `leaf_inverse`: each block is a diagonal of 0.8 to 1.25 plus independent entries off and on it. `front_inverse`: each block is a diagonal of 0.8 to 1.25 plus independent entries off and on it.
All inputs are finite; a program needn't handle non-finite values.
Results may differ from a plain program's by a relative error of at most 0.00016.
Values sent between devices are 32-bit elements; how exact they have to be, the bound alone decides.
A program may use at most 64 MiB of HBM per device.

v0:
```python
import jax
import jax.numpy as jnp
from jax import lax
from jax.sharding import PartitionSpec as P

highest = lax.Precision.HIGHEST


def from_root(block, axis, source):
    block = jnp.where(lax.axis_index(axis) == source, block, jnp.zeros_like(block))
    return lax.psum(block, axis)


def on_device(
    leaf_rhs, front_rhs, leaf_inverse, coupling, front_factor, front_inverse, parent, rows
):
    leaf_me = lax.axis_index("leaf")
    slot_me = lax.axis_index("front")
    groups = lax.axis_size("front")
    panel_rows = front_inverse.shape[2]
    leaf_inv = leaf_inverse[0, 0]
    coupling_block = coupling[0, 0]
    parent_me = parent[0, 0]
    factor_rows = front_factor[0]
    block_inv = front_inverse[0]
    iota_panel = jnp.arange(panel_rows, dtype=jnp.int32)
    own_onehot = (rows[0, 0][:, None] == iota_panel[None, :]).astype(jnp.float32)

    def add_children(pieces):
        upd_piece, parent_piece, rows_piece = pieces
        chosen = (parent_piece[:, 0] == leaf_me).astype(jnp.float32)
        onehot = (rows_piece[:, :, None] == iota_panel[None, None, :]).astype(jnp.float32)
        weighted = upd_piece * chosen[:, None, None, None]
        return jnp.einsum("kbrc,kcp->brp", weighted, onehot, precision=highest)

    def pick_parent(piece):
        sources = jnp.arange(piece.shape[0], dtype=jnp.int32)
        chosen = (sources == parent_me).astype(jnp.float32)
        return jnp.einsum("kbrp,k->brp", piece, chosen, precision=highest)

    def solve(rhs_block, front_block):
        leaf_y = jnp.einsum("brs,ts->brt", rhs_block, leaf_inv, precision=highest)
        update = jnp.einsum("brs,cs->brc", leaf_y, coupling_block, precision=highest)
        children = add_children(
            (
                lax.all_gather(update[None], "leaf", axis=0, tiled=True),
                lax.all_gather(parent, "leaf", axis=0, tiled=True),
                lax.all_gather(rows[:, 0], "leaf", axis=0, tiled=True),
            )
        )
        front_load = front_block - children
        pending = front_load
        front_y = jnp.zeros_like(front_load)
        for block_id in range(groups):
            solved_here = jnp.einsum("brq,pq->brp", pending, block_inv, precision=highest)
            received = from_root(solved_here, "front", block_id)
            from_below = jnp.einsum(
                "brq,pq->brp",
                received,
                factor_rows[:, block_id * panel_rows : (block_id + 1) * panel_rows],
                precision=highest,
            )
            pending = jnp.where(slot_me > block_id, pending - from_below, pending)
            front_y = jnp.where(slot_me == block_id, received, front_y)
        pending = front_y
        front_x = jnp.zeros_like(front_y)
        for block_id in reversed(range(groups)):
            solved_here = jnp.einsum("brp,pq->brq", pending, block_inv, precision=highest)
            spread = jnp.einsum("brp,pf->brf", solved_here, factor_rows, precision=highest)
            spread = from_root(spread, "front", block_id)
            from_above = lax.dynamic_slice_in_dim(spread, slot_me * panel_rows, panel_rows, 2)
            front_x = jnp.where(slot_me == block_id, solved_here, front_x)
            pending = jnp.where(slot_me < block_id, pending - from_above, pending)
        parent_panel = pick_parent(lax.all_gather(front_x[None], "leaf", axis=0, tiled=True))
        gathered_rows = jnp.einsum("brp,cp->brc", parent_panel, own_onehot, precision=highest)
        remain = leaf_y - jnp.einsum(
            "brc,cs->brs", gathered_rows, coupling_block, precision=highest
        )
        leaf_x = jnp.einsum("brt,ts->brs", remain, leaf_inv, precision=highest)
        return (leaf_x, front_x)

    leaf_flat = leaf_rhs[:, :, 0, 0, :]
    front_flat = front_rhs[:, :, 0, :]
    outcomes = [
        solve(leaf_flat[batch_id : batch_id + 1], front_flat[batch_id : batch_id + 1])
        for batch_id in range(leaf_flat.shape[0])
    ]
    leaf_x = jnp.concatenate([outcome[0] for outcome in outcomes], axis=0)
    front_x = jnp.concatenate([outcome[1] for outcome in outcomes], axis=0)
    return (leaf_x[:, :, None, None, :], front_x[:, :, None, :])


def solution(mesh):
    placed = (
        P(None, None, "leaf", "front", None),
        P(None, None, "leaf", "front"),
        P("leaf", "front", None, None),
        P("leaf", "front", None, None),
        P("leaf", "front", None),
        P("leaf", "front", None),
        P("leaf", "front"),
        P("leaf", "front", None),
    )
    return jax.shard_map(
        on_device,
        mesh=mesh,
        in_specs=placed,
        out_specs=(P(None, None, "leaf", "front", None), P(None, None, "leaf", "front")),
        check_vma=False,
    )
```

profile of v0, /device:TPU:0, one launch (start us, length us, event | category | flops | bytes accessed | tf_op | source)
XLA Modules:
  0.0 505.5 jit_solution(10093249944751546976)
XLA Ops:
  7.2 0.0 copy-start
  7.2 0.0 all-gather.14.cloned.1.call-start
  7.2 0.9 fusion.99
  8.1 1.3 fusion.57
  9.4 2.1 fusion.49
  11.5 0.0 all-gather.14.cloned.1.call-update
  11.5 0.0 all-gather.10.cloned.1.call-start
  11.6 1.3 fusion.60
  12.9 2.1 fusion.52
  15.0 0.0 all-gather.10.cloned.1.call-update
  15.0 0.0 all-reduce.12.cloned.1.call-start
  15.7 179.3 %all-gather.1 = s32[64,1,384]{2,1,0:T(1,128)S(1)} all-gather(s32[1,1,384]{2,1,0:T(1,128)} %param.15), channel_id=3, replica_groups=mesh['leaf'=64,'front'=2] {'leaf'}, dimensions={0}, use_global_device_ids=true | all-gather | bytes 99840 | tf_op jit(solution)/shard_map/all_gather | solution.py:48
  195.0 1.3 dynamic-slice
  196.3 0.7 bitcast_dynamic-update-slice_fusion
  197.0 15.5 %all-reduce = s32[64]{0:T(128)S(1)} all-reduce(s32[64]{0:T(128)S(1)} %bitcast_dynamic-update-slice_fusion), channel_id=1, replica_groups=mesh['leaf'=64,'front'=2] {'leaf'}, use_global_device_ids=true, to_apply=%add | all-reduce | flops 64 | bytes 512
  212.5 0.9 fusion.98
  213.4 0.0 all-gather.14.cloned.1.call-done
  213.5 21.3 %fusion.28 = f32[32,512]{1,0:T(8,128)S(1)} fusion(s32[64,384]{1,0:T(8,128)S(1)} %bitcast.159, f32[64,1,32,384]{3,2,0,1:T(8,128)} %bitcast.161, f32[64]{0:T(128)S(1)} %compare_convert_fusion, f32[1,32,1,512]{3,2,1,0:T(1,128)S(1)} %get-tuple-element.13), kind=kOutput, calls=%fused_computation.35 | convolution fusion | flops 4845223936 | bytes 3375360 | tf_op jit(solution)/shard_map/kbrc,kcp->brp/dot_general | solution.py:34
  234.7 0.0 all-gather.10.cloned.1.call-done
  234.8 21.3 %fusion.31 = f32[32,512]{1,0:T(8,128)S(1)} fusion(s32[64,384]{1,0:T(8,128)S(1)} %bitcast.160, f32[64,1,32,384]{3,2,0,1:T(8,128)} %bitcast.162, f32[64]{0:T(128)S(1)} %compare_convert_fusion, f32[1,32,1,512]{3,2,1,0:T(1,128)S(1)} %get-tuple-element.12), kind=kOutput, calls=%fused_computation.36 | convolution fusion | flops 4845223936 | bytes 3375360 | tf_op jit(solution)/shard_map/kbrc,kcp->brp/dot_general | solution.py:34
  256.1 0.0 copy-done
  256.1 0.0 copy-start.1
  256.1 1.7 fusion.24
  257.8 1.7 fusion.27
  259.5 0.0 all-reduce.12.cloned.1.call-update
  259.5 0.0 all-reduce.10.cloned.1.call-start
  259.5 25.4 %all-reduce.12.cloned.1.call-done = (f32[1,32,512]{2,1,0:T(8,128)}, f32[1,32,512]{2,1,0:T(8,128)}) async-done(((f32[1,32,512]{2,1,0:T(8,128)}, f32[1,32,512]{2,1,0:T(8,128)}), (f32[1,32,512]{2,1,0:T(8,128)}, f32[1,32,512]{2,1,0:T(8,128)})) %all-reduce.12.cloned.1.call-update) | async-done | bytes 131088 | tf_op jit(solution)/shard_map/psum | solution.py:11
  285.0 0.0 copy-done.1
  285.0 2.0 fusion.26
  286.9 1.9 fusion.23
  288.8 0.0 copy-start.4
  288.9 1.7 fusion.25
  290.5 1.7 fusion.22
  292.2 0.0 all-reduce.10.cloned.1.call-update
  292.2 0.2 all-reduce.8.cloned.1.call-start
  292.5 24.8 %all-reduce.10.cloned.1.call-done = (f32[1,32,512]{2,1,0:T(8,128)}, f32[1,32,512]{2,1,0:T(8,128)}) async-done(((f32[1,32,512]{2,1,0:T(8,128)}, f32[1,32,512]{2,1,0:T(8,128)}), (f32[1,32,512]{2,1,0:T(8,128)}, f32[1,32,512]{2,1,0:T(8,128)})) %all-reduce.10.cloned.1.call-update) | async-done | bytes 131088 | tf_op jit(solution)/shard_map/psum | solution.py:11
  317.3 0.0 copy-done.5
  317.3 0.7 fusion.40
  318.0 2.0 fusion.15
  320.0 0.0 copy-done.4
  320.0 0.7 fusion.35
  320.7 2.0 fusion.14
  322.7 0.0 all-reduce.8.cloned.1.call-update
  322.7 0.0 all-gather.12.cloned.1.call-start
  322.8 26.1 %all-reduce.8.cloned.1.call-done = (f32[1,32,1024]{2,1,0:T(8,128)}, f32[1,32,1024]{2,1,0:T(8,128)}) async-done(((f32[1,32,1024]{2,1,0:T(8,128)}, f32[1,32,1024]{2,1,0:T(8,128)}), (f32[1,32,1024]{2,1,0:T(8,128)}, f32[1,32,1024]{2,1,0:T(8,128)})) %all-reduce.8.cloned.1.call-update) | async-done | bytes 262160 | tf_op jit(solution)/shard_map/psum | solution.py:11
  348.9 2.2 convolution_select_fusion.5
  351.0 0.0 all-gather.12.cloned.1.call-update
  351.1 0.0 all-gather.16.cloned.1.call-start
  351.1 0.0 copy-start.2
  351.1 2.2 convolution_select_fusion.2
  353.4 0.0 all-gather.16.cloned.1.call-update
  353.4 0.9 maximum_bitcast_fusion
  354.3 0.8 copy.17
  355.1 66.5 %all-gather.12.cloned.1.call-done = f32[2048,512]{1,0:T(8,128)} async-done(((f32[32,512]{1,0:T(8,128)}), f32[2048,512]{1,0:T(8,128)}) %all-gather.12.cloned.1.call-update) | async-done | bytes 4194320 | tf_op jit(solution)/shard_map/all_gather | solution.py:74
  421.6 5.8 %fusion.6 = f32[1,32,512]{2,0,1:T(1,128)S(1)} fusion(f32[64,32,512]{2,1,0:T(8,128)} %bitcast.155, s32[]{:T(128)} %bitcast.151), kind=kOutput, calls=%fused_computation.7 | convolution fusion | flops 12582976 | bytes 4259844 | tf_op jit(solution)/shard_map/kbrp,k->brp/dot_general | solution.py:39
  427.4 0.6 fusion.47
  427.9 0.3 convolution_subtract_fusion.3
  428.3 0.2 convolution_bitcast_fusion.1
  428.5 62.5 %all-gather.16.cloned.1.call-done = f32[2048,512]{1,0:T(8,128)} async-done(((f32[32,512]{1,0:T(8,128)}), f32[2048,512]{1,0:T(8,128)}) %all-gather.16.cloned.1.call-update) | async-done | bytes 4194320 | tf_op jit(solution)/shard_map/all_gather | solution.py:74
  491.0 5.8 %fusion.4 = f32[1,32,512]{2,0,1:T(1,128)S(1)} fusion(f32[64,32,512]{2,1,0:T(8,128)} %bitcast.156, s32[]{:T(128)} %bitcast.152), kind=kOutput, calls=%fused_computation.5 | convolution fusion | flops 12582976 | bytes 4259844 | tf_op jit(solution)/shard_map/kbrp,k->brp/dot_general | solution.py:39
  496.8 0.5 fusion.46
  497.4 0.3 convolution_subtract_fusion.2
  497.7 0.2 convolution_bitcast_fusion
  498.0 0.7 copy.16
  (13 shorter events, 0.1 us)
Async XLA Ops:
  7.2 248.9 %copy-start = (f32[1,512,512]{2,1,0:T(8,128)S(1)}, f32[1,512,512]{2,1,0:T(8,128)}, u32[]{:S(2)}) copy-start(f32[1,512,512]{2,1,0:T(8,128)} %param.13) | copy-start | bytes 3145732
  7.2 206.3 %all-gather.14.cloned.1.call-start = ((), (), s32[]{:S(2)}) async-start(), calls=%async_computation.2 | async-start | bytes 3194880 | tf_op jit(solution)/shard_map/all_gather | solution.py:46
  11.5 223.3 %all-gather.10.cloned.1.call-start = ((), (), s32[]{:S(2)}) async-start(), calls=%async_computation | async-start | bytes 3194880 | tf_op jit(solution)/shard_map/all_gather | solution.py:46
  15.0 270.0 %all-reduce.12.cloned.1.call-start = ((), (), s32[]{:S(2)}) async-start(), calls=%async_computation.6 | async-start | bytes 262144 | tf_op jit(solution)/shard_map/psum | solution.py:11
  256.1 28.9 %copy-start.1 = (f32[1,512,1024]{2,1,0:T(8,128)S(1)}, f32[1,512,1024]{2,1,0:T(8,128)}, u32[]{:S(2)}) copy-start(f32[1,512,1024]{2,1,0:T(8,128)} %param.12) | copy-start | bytes 6291460
  259.5 57.8 %all-reduce.10.cloned.1.call-start = ((), (), s32[]{:S(2)}) async-start(), calls=%async_computation.5 | async-start | bytes 262144 | tf_op jit(solution)/shard_map/psum | solution.py:11
  285.0 32.3 %copy-start.5 = (f32[1,32,512]{2,1,0:T(8,128)S(1)}, f32[1,32,512]{2,1,0:T(8,128)}, u32[]{:S(2)}) copy-start(f32[1,32,512]{2,1,0:T(8,128)} %get-tuple-element.11) | copy-start | bytes 196612
  288.8 31.2 %copy-start.4 = (f32[1,32,512]{2,1,0:T(8,128)S(1)}, f32[1,32,512]{2,1,0:T(8,128)}, u32[]{:S(2)}) copy-start(f32[1,32,512]{2,1,0:T(8,128)} %get-tuple-element.10) | copy-start | bytes 196612
  292.2 56.6 %all-reduce.8.cloned.1.call-start = ((), (), s32[]{:S(2)}) async-start(), calls=%async_computation.4 | async-start | bytes 524288 | tf_op jit(solution)/shard_map/psum | solution.py:11
  317.3 2.7 copy-start.6
  320.0 33.4 %copy-start.7 = (s32[1,1,384]{2,1,0:T(1,128)S(1)}, s32[1,1,384]{2,1,0:T(1,128)}, u32[]{:S(2)}) copy-start(s32[1,1,384]{2,1,0:T(1,128)} %param.15) | copy-start | bytes 4612
  322.7 98.9 %all-gather.12.cloned.1.call-start = ((), (), s32[]{:S(2)}) async-start(), calls=%async_computation.1 | async-start | bytes 4259840 | tf_op jit(solution)/shard_map/all_gather | solution.py:74
  351.1 140.0 %all-gather.16.cloned.1.call-start = ((), (), s32[]{:S(2)}) async-start(), calls=%async_computation.3 | async-start | bytes 4259840 | tf_op jit(solution)/shard_map/all_gather | solution.py:74
  351.1 76.8 %copy-start.2 = (f32[1,1,384,256]{3,2,1,0:T(8,128)S(1)}, f32[1,1,384,256]{3,2,1,0:T(8,128)}, u32[]{:S(2)}) copy-start(f32[1,1,384,256]{3,2,1,0:T(8,128)} %param.11) | copy-start | bytes 1179652
  353.4 74.9 %copy-start.3 = (f32[1,1,256,256]{3,2,1,0:T(8,128)S(1)}, f32[1,1,256,256]{3,2,1,0:T(8,128)}, u32[]{:S(2)}) copy-start(f32[1,1,256,256]{3,2,1,0:T(8,128)} %param.10) | copy-start | bytes 786436
Sparse Core Ops, SparseCore 0:
  11.6 69.6 all-gather.13
  84.6 64.4 all-gather.9
  259.6 25.3 all-reduce.11
  292.4 24.9 all-reduce.9
  322.8 25.9 all-reduce.7
  351.6 69.9 all-gather.11
  425.0 65.9 all-gather.15
where the time goes:
time: 506 us; the launch traced here: 505 us
  waiting for transfers between devices  206 us (41%)
  blocking collectives  195 us (39%)
  matrix products  83.4 us (16%)
  between operations  15 us (3%)
  local copies, waits for them, and re-layouts  5.29 us (1%)
    all_gather x1, blocking collectives, solve(): lax.all_gather(rows[:, 0], 'leaf', axis=0, tiled=True)  179 us
    all_gather x2, waiting for transfers between devices, solve(): lax.all_gather(front_x[None], 'leaf', axis=0, tiled=True)  129 us
    psum x3, waiting for transfers between devices, from_root(): return lax.psum(block, axis)  76.4 us
    dot_general x2, matrix products, add_children(): return jnp.einsum('kbrc,kcp->brp', weighted, onehot, precision=highest)  42.6 us
    unnamed x1, blocking collectives  15.5 us
    dot_general x2, matrix products, pick_parent(): return jnp.einsum('kbrp,k->brp', piece, chosen, precision=highest)  11.5 us
  transfers between devices with their start and end apart: 7, of which 5 were waited for; matrix products, arithmetic and copies ran while one was open for 8% of the time, Pallas kernels for 0%

commit v1 on v0

v1 whole, which is shorter than its diff:
```python
import jax
import jax.numpy as jnp
from jax import lax
from jax.experimental import pallas as pl
from jax.experimental.pallas import tpu as pltpu
from jax.sharding import PartitionSpec as P

MESH = pl.DeviceIdType.MESH
NN = (((1,), (0,)), ((), ()))
NT = (((1,), (1,)), ((), ()))
TN = (((0,), (0,)), ((), ()))
F32, BF16 = jnp.float32, jnp.bfloat16
LANES = 128
GROUP = 8


def split(value):
    high = value.astype(BF16)
    return high, (value - high.astype(F32)).astype(BF16)


def dot(a, b, dims):
    return lax.dot_general(a, b, dims, preferred_element_type=F32)


def dot3(a, b, dims):
    (a_high, a_low), (b_high, b_low) = a, b
    small = dot(a_high, b_low, dims) + dot(a_low, b_high, dims)
    return dot(a_high, b_high, dims) + small


def kernel(
    leaf_rhs, front_rhs, leaf_inv, coupling, factor, inverse, parent, rows,
    leaf_out, front_out,
    rhs_v, load_v, linv_v, coup_v, rows_v, inv0_v, inv1_v, fact_v,
    par_v, recv1, send2, recv2, recv3, send4, recv4, loads,
    inv0_s, inv1_s, fact_s, p_s, g_s, other_s, own_s, last_s,
    in_sem, par_out, par_in, core_out, core_in, load_out, load_in,
    out1, in1, out2, in2, out3, in3, out4, in4,
):
    leaf, core = lax.axis_index("leaf"), lax.axis_index("front")
    panel = inv0_v.shape[0]
    half = recv1.shape[2]
    z, y, x = leaf // 16, (leaf // 4) % 4, leaf % 4

    def near(c):
        return c + 1 - 2 * (c % 2)

    def across(c):
        return 3 - c

    peers = []
    for step in (near, across):
        sx, sy, sz = step(x), step(y), step(z)
        peers.append(
            [
                (sz if k & 4 else z) * 16 + (sy if k & 2 else y) * 4 + (sx if k & 1 else x)
                for k in range(GROUP)
            ]
        )

    def local(src, dst, place):
        return pltpu.make_async_copy(src, dst, in_sem.at[place])

    loads_in = [
        local(leaf_rhs, rhs_v, 0),
        local(leaf_inv, linv_v, 1),
        local(coupling, coup_v, 2),
        local(rows, rows_v, 3),
        local(front_rhs, load_v, 4),
    ]
    for copy in loads_in:
        copy.start()
    left_part = factor.at[:, pl.ds(0, panel)]

    barrier = pltpu.get_barrier_semaphore()
    for group in peers:
        for peer in group[1:]:
            pl.semaphore_signal(barrier, inc=1, device_id=(peer, core), device_id_type=MESH)
    pl.semaphore_signal(barrier, inc=1, device_id=(leaf, 1 - core), device_id_type=MESH)

    @pl.when(core == 0)
    def _():
        local(inverse, inv0_v, 5).start()

    @pl.when(core == 1)
    def _():
        local(inverse, inv1_v, 5).start()
        local(left_part, fact_v, 6).start()

    def remote(src, dst, out_sem, into_sem, peer, side):
        return pltpu.make_async_remote_copy(
            src_ref=src, dst_ref=dst, send_sem=out_sem, recv_sem=into_sem,
            device_id=(peer, side), device_id_type=MESH,
        )

    own_parent = jnp.full((8, LANES), parent[0, 0], jnp.int32)
    par_v[0, 0] = own_parent
    par_v[1, 0] = own_parent
    loads_in[0].wait()
    loads_in[1].wait()
    count = 2 * half
    rhs = jnp.concatenate(
        [rhs_v[pl.ds(0, count, stride=2), :], rhs_v[pl.ds(1, count, stride=2), :]], axis=1
    )
    leaf_inv_parts = split(linv_v[...])
    leaf_y = dot3(split(rhs), leaf_inv_parts, NT)
    leaf_y_parts = split(leaf_y)
    loads_in[2].wait()
    loads_in[3].wait()
    coupling_parts = split(coup_v[...])
    update = dot3(leaf_y_parts, coupling_parts, NT)
    sublane = lax.broadcasted_iota(jnp.int32, (panel, rows_v.shape[1]), 0)
    spread_to = (sublane == rows_v[...]).astype(F32).astype(BF16)
    update_high, update_low = split(update)
    message = dot(update_high, spread_to, NT) + dot(update_low, spread_to, NT)
    for h in range(2):
        recv1[h, 0] = message[h * half : (h + 1) * half]

    pl.semaphore_wait(barrier, 2 * (GROUP - 1) + 1)

    sent = []

    def exchange(h, group, source, target, out_sem, into_sem):
        copies = [None]
        for k in range(1, GROUP):
            copy = remote(source(h, k), target.at[h, k], out_sem.at[h, k], into_sem.at[h, k], peers[group][k], core)
            copy.start()
            copies.append(copy)
        sent.extend(copies[1:])
        return copies

    tables = [
        exchange(h, h, lambda h, k: par_v.at[h, 0], par_v, par_out, par_in) for h in range(2)
    ]
    first = [
        exchange(h, h, lambda h, k: recv1.at[h, 0], recv1, out1, in1) for h in range(2)
    ]

    def core_copy(src, dst, place):
        return remote(src, dst, core_out.at[place], core_in.at[place], leaf, 1 - core)

    @pl.when(core == 0)
    def _():
        core_copy(inverse, inv0_v, 0).start()

    @pl.when(core == 1)
    def _():
        core_copy(inverse, inv1_v, 1).start()
        core_copy(left_part, fact_v, 2).start()

    base = dot3(leaf_y_parts, leaf_inv_parts, NN)
    both = split(dot3(coupling_parts, leaf_inv_parts, NN))
    last = split(dot(spread_to, both[0], NN) + dot(spread_to, both[1], NN))
    last_s[0] = last[0]
    last_s[1] = last[1]

    block = 128

    def keep(where, value, at):
        high, low = split(value)
        where[0, at, :] = high
        where[1, at, :] = low

    def spans(i):
        return pl.ds(pl.multiple_of(i * block, block), block)

    def whole(ref):
        return ref[0], ref[1]

    def by_rows(ref, at):
        return ref[0, at, :], ref[1, at, :]

    def by_columns(ref, at):
        return ref[0, :, at], ref[1, :, at]

    def over(body):
        @pl.loop(0, panel // block)
        def _(i):
            body(spans(i))

    @pl.when(core == 0)
    def _():
        local(inverse, inv0_v, 5).wait()
        core_copy(inverse, inv1_v, 1).wait_recv()
        core_copy(left_part, fact_v, 2).wait_recv()

    @pl.when(core == 1)
    def _():
        local(inverse, inv1_v, 5).wait()
        local(left_part, fact_v, 6).wait()
        core_copy(inverse, inv0_v, 0).wait_recv()

    def split_all(at):
        keep(inv0_s, inv0_v[at, :], at)
        keep(inv1_s, inv1_v[at, :], at)
        keep(fact_s, fact_v[at, :], at)

    over(split_all)
    over(lambda at: keep(p_s, dot3(by_rows(fact_s, at), whole(inv0_s), NN), at))
    over(lambda at: keep(g_s, dot3(by_columns(inv1_s, at), whole(inv1_s), TN), at))

    @pl.when(core == 0)
    def _():
        over(lambda at: keep(other_s, -dot3(by_rows(g_s, at), whole(p_s), NN), at))

    @pl.when(core == 1)
    def _():
        over(lambda at: keep(other_s, -dot3(by_columns(p_s, at), whole(g_s), TN), at))

    groups_of_rows = half // 8

    def sums(source, h, group, into_own, into_others):
        @pl.loop(0, groups_of_rows)
        def _(i):
            at = pl.ds(pl.multiple_of(i * 8, 8), 8)
            marks = [par_v[h, k] for k in range(GROUP)]
            for c in range(panel // LANES):
                lanes = pl.ds(c * LANES, LANES)
                values = [source[h, k, at, lanes] for k in range(GROUP)]
                for j in range(GROUP):
                    total = jnp.zeros((8, LANES), F32)
                    for k in range(GROUP):
                        total = total + jnp.where(marks[k] == peers[group][j], values[k], 0.0)
                    if j == 0:
                        into_own[h, 0, at, lanes] = total
                    else:
                        into_others[h, j, at, lanes] = total

    second = []
    for h in range(2):
        for k in range(1, GROUP):
            tables[h][k].wait_recv()
            first[h][k].wait_recv()
        sums(recv1, h, 1 - h, recv2, send2)
        second.append(exchange(h, 1 - h, lambda h, k: send2.at[h, k], recv2, out2, in2))

    @pl.when(core == 0)
    def _():
        def finish(at):
            value = dot3(by_columns(inv0_s, at), whole(inv0_s), TN)
            keep(own_s, value - dot3(by_columns(p_s, at), whole(other_s), TN), at)

        over(finish)

    @pl.when(core == 1)
    def _():
        def finish(at):
            own_s[0, at, :] = g_s[0, at, :]
            own_s[1, at, :] = g_s[1, at, :]

        over(finish)

    loads_in[4].wait()
    swaps, kept = [], []
    width = panel // LANES
    for h in range(2):
        for k in range(1, GROUP):
            second[h][k].wait_recv()
        total = recv2[h, 0]
        for k in range(1, GROUP):
            total = total + recv2[h, k]
        given = jnp.concatenate(
            [load_v[pl.ds(h * half * width + c, half, stride=width), :] for c in range(width)], axis=1
        )
        load = given - total
        loads[0, h] = load
        swap = remote(loads.at[0, h], loads.at[1, h], load_out.at[h], load_in.at[h], leaf, 1 - core)
        swap.start()
        swaps.append(swap)
        sent.append(swap)
        kept.append(dot3(split(load), whole(own_s), NN))
    third = []
    for h in range(2):
        swaps[h].wait_recv()
        solution = kept[h] + dot3(split(loads[1, h]), whole(other_s), NN)
        recv3[h, 0] = solution
        third.append(exchange(h, 1 - h, lambda h, k: recv3.at[h, 0], recv3, out3, in3))
        for c in range(width):
            front_out[pl.ds(h * half * width + c, half, stride=width), :] = solution[:, c * LANES : (c + 1) * LANES]

    def picks(h, group):
        @pl.loop(0, groups_of_rows)
        def _(i):
            at = pl.ds(pl.multiple_of(i * 8, 8), 8)
            marks = [par_v[h, k] for k in range(GROUP)]
            for c in range(panel // LANES):
                lanes = pl.ds(c * LANES, LANES)
                values = [recv3[h, j, at, lanes] for j in range(GROUP)]
                for k in range(GROUP):
                    picked = jnp.zeros((8, LANES), F32)
                    for j in range(GROUP):
                        picked = jnp.where(marks[k] == peers[group][j], values[j], picked)
                    if k == 0:
                        recv4[h, 0, at, lanes] = picked
                    else:
                        send4[h, k, at, lanes] = picked

    fourth = []
    for h in range(2):
        for k in range(1, GROUP):
            third[h][k].wait_recv()
        picks(h, 1 - h)
        fourth.append(exchange(h, h, lambda h, k: send4.at[h, k], recv4, out4, in4))

    for h in range(2):
        for k in range(1, GROUP):
            fourth[h][k].wait_recv()
        total = recv4[h, 0]
        for k in range(1, GROUP):
            total = total + recv4[h, k]
        result = base[h * half : (h + 1) * half] - dot3(split(total), whole(last_s), NN)
        for c in range(2):
            leaf_out[pl.ds(h * half * 2 + c, half, stride=2), :] = result[:, c * LANES : (c + 1) * LANES]

    for copy in sent:
        copy.wait_send()

    @pl.when(core == 0)
    def _():
        core_copy(inverse, inv0_v, 0).wait_send()

    @pl.when(core == 1)
    def _():
        core_copy(inverse, inv1_v, 1).wait_send()
        core_copy(left_part, fact_v, 2).wait_send()


def on_device(leaf_rhs, front_rhs, leaf_inverse, coupling, front_factor, front_inverse, parent, rows):
    batches, half = leaf_rhs.shape[:2]
    snode, panel = leaf_rhs.shape[4], front_rhs.shape[3]
    count, crows = batches * half, rows.shape[2]
    slots = pltpu.VMEM((2, GROUP, half, panel), F32)
    square = pltpu.VMEM((panel, panel), F32)
    pair = pltpu.VMEM((2, panel, panel), BF16)
    dma = pltpu.SemaphoreType.DMA
    by_group = dma((2, GROUP))
    hbm, vmem = pl.BlockSpec(memory_space=pl.ANY), pl.BlockSpec(memory_space=pltpu.VMEM)
    leaf_x, front_x = pl.pallas_call(
        kernel,
        out_shape=(
            jax.ShapeDtypeStruct((count * snode // LANES, LANES), F32),
            jax.ShapeDtypeStruct((count * panel // LANES, LANES), F32),
        ),
        in_specs=[hbm] * 6 + [pl.BlockSpec(memory_space=pltpu.SMEM), hbm],
        out_specs=(vmem, vmem),
        scratch_shapes=[
            pltpu.VMEM((count * snode // LANES, LANES), F32),
            pltpu.VMEM((count * panel // LANES, LANES), F32),
            pltpu.VMEM((snode, snode), F32),
            pltpu.VMEM((crows, snode), F32),
            pltpu.VMEM((1, crows), jnp.int32),
            square, square, square,
            pltpu.VMEM((2, GROUP, 8, LANES), jnp.int32),
            slots, slots, slots, slots, slots, slots,
            pltpu.VMEM((2, 2, half, panel), F32),
            pair, pair, pair, pair, pair, pair, pair,
            pltpu.VMEM((2, panel, snode), BF16),
            dma((7,)), by_group, by_group, dma((3,)), dma((3,)), dma((2,)), dma((2,)),
        ] + [by_group] * 8,
        compiler_params=pltpu.CompilerParams(
            collective_id=0, has_side_effects=True, vmem_limit_bytes=50 << 20
        ),
    )(
        leaf_rhs.reshape(count * snode // LANES, LANES),
        front_rhs.reshape(count * panel // LANES, LANES),
        leaf_inverse[0, 0],
        coupling[0, 0],
        front_factor[0],
        front_inverse[0],
        parent,
        rows[0],
    )
    return (
        leaf_x.reshape(batches, half, 1, 1, snode),
        front_x.reshape(batches, half, 1, panel),
    )


def solution(mesh):
    placed = (
        P(None, None, "leaf", "front", None),
        P(None, None, "leaf", "front"),
        P("leaf", "front", None, None),
        P("leaf", "front", None, None),
        P("leaf", "front", None),
        P("leaf", "front", None),
        P("leaf", "front"),
        P("leaf", "front", None),
    )
    return jax.shard_map(
        on_device,
        mesh=mesh,
        in_specs=placed,
        out_specs=(P(None, None, "leaf", "front", None), P(None, None, "leaf", "front")),
        check_vma=False,
    )
```

time: 506 us -> 59.3 us (0.12)
  waiting for transfers between devices: 206 us -> 0 us
  blocking collectives: 195 us -> 0 us
  matrix products: 83.4 us -> 0 us
  Pallas kernels: 0 us -> 50.5 us
  between operations: 15 us -> 1.3 us
    all_gather x1 -> x0, blocking collectives: 179 us -> none  [solve(): lax.all_gather(rows[:, 0], 'leaf', axis=0, tiled=True)]
    all_gather x4 -> x0, waiting for transfers between devices: 129 us -> none  [the longest x2 129 us: solve(): lax.all_gather(front_x[None], 'leaf', axis=0, tiled=True)]
    dot_general x26 -> x0, matrix products: 83.4 us -> none  [the longest x2 42.6 us: add_children(): return jnp.einsum('kbrc,kcp->brp', weighted, onehot, precision=highest)]
    psum x3 -> x0, waiting for transfers between devices: 76.4 us -> none  [from_root(): return lax.psum(block, axis)]
    pallas_call x0 -> x1, Pallas kernels: none -> 50.5 us  [on_device(): pl.pallas_call(kernel, out_shape=(jax.ShapeDtypeStruct((count * snode //...]
    unnamed x1 -> x0, blocking collectives: 15.5 us -> none
  transfers between devices with their start and end apart: 7 -> 0, of which waited for: 5 -> 0; matrix products, arithmetic and copies ran while one was open for 8% -> 0% of each run, Pallas kernels for 0% -> 0%
where the time goes in v1:
time: 59.3 us; the launch traced here: 58.6 us
  Pallas kernels  50.5 us (85%)
  local copies, waits for them, and re-layouts  6.87 us (12%)
  between operations  1.3 us (2%)
    pallas_call x1, Pallas kernels, on_device(): pl.pallas_call(kernel, out_shape=(jax.ShapeDtypeStruct((count * snode //...  50.5 us
    unnamed x14, local copies, waits for them, and re-layouts  6.87 us

profile of v1, /device:TPU:0, one launch (start us, length us, event | category | flops | bytes accessed | tf_op | source)
XLA Modules:
  0.0 58.6 jit_solution(6895196481118394809)
XLA Ops:
  1.3 0.0 copy-start
  1.3 1.2 %copy-done = f32[1,512,512]{2,1,0:T(8,128)S(1)} copy-done((f32[1,512,512]{2,1,0:T(8,128)S(1)}, f32[1,512,512]{2,1,0:T(8,128)}, u32[]{:S(2)}) %copy-start) | copy-done | bytes 1048600
  2.5 0.0 copy-start.1
  2.5 1.0 %copy-done.1 = f32[1,1,384,256]{3,2,1,0:T(8,128)S(1)} copy-done((f32[1,1,384,256]{3,2,1,0:T(8,128)S(1)}, f32[1,1,384,256]{3,2,1,0:T(8,128)}, u32[]{:S(2)}) %copy-start.1) | copy-done | bytes 393240
  3.5 0.0 copy-start.2
  3.5 0.9 %copy-done.2 = f32[1,1,256,256]{3,2,1,0:T(8,128)S(1)} copy-done((f32[1,1,256,256]{3,2,1,0:T(8,128)S(1)}, f32[1,1,256,256]{3,2,1,0:T(8,128)}, u32[]{:S(2)}) %copy-start.2) | copy-done | bytes 262168
  4.5 0.0 copy-start.3
  4.5 0.9 %copy-done.3 = f32[2,32,1,512]{3,2,1,0:T(1,128)S(1)} copy-done((f32[2,32,1,512]{3,2,1,0:T(1,128)S(1)}, f32[2,32,1,512]{3,2,1,0:T(1,128)}, u32[]{:S(2)}) %copy-start.3) | copy-done | bytes 131096
  5.4 0.0 copy-start.4
  5.4 0.8 %copy-done.4 = f32[2,32,1,1,256]{4,3,2,1,0:T(1,128)S(1)} copy-done((f32[2,32,1,1,256]{4,3,2,1,0:T(1,128)S(1)}, f32[2,32,1,1,256]{4,3,2,1,0:T(1,128)}, u32[]{:S(2)}) %copy-start.4) | copy-done | bytes 65560
  6.2 0.0 copy-start.5
  6.2 0.7 %copy-done.5 = s32[1,1,384]{2,1,0:T(1,128)S(1)} copy-done((s32[1,1,384]{2,1,0:T(1,128)S(1)}, s32[1,1,384]{2,1,0:T(1,128)}, u32[]{:S(2)}) %copy-start.5) | copy-done | bytes 1560
  6.9 50.5 %shard_map.95 = (f32[128,128]{1,0:T(8,128)S(1)}, f32[256,128]{1,0:T(8,128)S(1)}) custom-call(f32[128,128]{1,0:T(8,128)S(1)} %bitcast.14, f32[256,128]{1,0:T(8,128)S(1)} %bitcast.12, f32[256,256]{1,0:T(8,128)S(1)} %bitcast.11, f32[384,256]{1,0:T(8,128)S(1)} %bitcast.10, f32[512,1024]{1,0:T(8,128)} %bitcast.17, f32[512,512]{1,0:T(8,128)S(1)} %bitcast.9, ...), custom_call_target="tpu_custom_call" | custom-call | tf_op jit(solution)/shard_map/pallas_call | solution.py:339
  57.3 0.6 %copy.15 = f32[2,32,1,1,256]{4,3,2,1,0:T(1,128)} copy(f32[2,32,1,1,256]{4,3,2,1,0:T(1,128)S(1)} %bitcast.15) | data formatting | bytes 131072
  58.0 0.7 %copy.16 = f32[2,32,1,512]{3,2,1,0:T(1,128)} copy(f32[2,32,1,512]{3,2,1,0:T(1,128)S(1)} %bitcast.13) | data formatting | bytes 262144
Async XLA Ops:
  1.3 1.2 %copy-start = (f32[1,512,512]{2,1,0:T(8,128)S(1)}, f32[1,512,512]{2,1,0:T(8,128)}, u32[]{:S(2)}) copy-start(f32[1,512,512]{2,1,0:T(8,128)} %param.13) | copy-start | bytes 3145732
  2.5 1.0 %copy-start.1 = (f32[1,1,384,256]{3,2,1,0:T(8,128)S(1)}, f32[1,1,384,256]{3,2,1,0:T(8,128)}, u32[]{:S(2)}) copy-start(f32[1,1,384,256]{3,2,1,0:T(8,128)} %param.11) | copy-start | bytes 1179652
  3.5 0.9 %copy-start.2 = (f32[1,1,256,256]{3,2,1,0:T(8,128)S(1)}, f32[1,1,256,256]{3,2,1,0:T(8,128)}, u32[]{:S(2)}) copy-start(f32[1,1,256,256]{3,2,1,0:T(8,128)} %param.10) | copy-start | bytes 786436
  4.5 0.9 %copy-start.3 = (f32[2,32,1,512]{3,2,1,0:T(1,128)S(1)}, f32[2,32,1,512]{3,2,1,0:T(1,128)}, u32[]{:S(2)}) copy-start(f32[2,32,1,512]{3,2,1,0:T(1,128)} %param.9) | copy-start | bytes 393220
  5.4 0.8 %copy-start.4 = (f32[2,32,1,1,256]{4,3,2,1,0:T(1,128)S(1)}, f32[2,32,1,1,256]{4,3,2,1,0:T(1,128)}, u32[]{:S(2)}) copy-start(f32[2,32,1,1,256]{4,3,2,1,0:T(1,128)} %param.8) | copy-start | bytes 196612
  6.2 0.7 %copy-start.5 = (s32[1,1,384]{2,1,0:T(1,128)S(1)}, s32[1,1,384]{2,1,0:T(1,128)}, u32[]{:S(2)}) copy-start(s32[1,1,384]{2,1,0:T(1,128)} %param.15) | copy-start | bytes 4612

commit v2 on v1

v2 whole, which is shorter than its diff:
```python
import jax
import jax.numpy as jnp
from jax import lax
from jax.experimental import pallas as pl
from jax.experimental.pallas import tpu as pltpu
from jax.sharding import PartitionSpec as P

MESH = pl.DeviceIdType.MESH
NN = (((1,), (0,)), ((), ()))
NT = (((1,), (1,)), ((), ()))
TN = (((0,), (0,)), ((), ()))
F32, BF16 = jnp.float32, jnp.bfloat16
LANES = 128
GROUP = 8
UNITS = 4
NEXT = (1, 2, 4)
RELAYS = ((2, 1, 3), (4, 2, 6), (1, 4, 5))


def split(value):
    high = value.astype(BF16)
    return high, (value - high.astype(F32)).astype(BF16)


def dot(a, b, dims):
    return lax.dot_general(a, b, dims, preferred_element_type=F32)


def dot3(a, b, dims):
    (a_high, a_low), (b_high, b_low) = a, b
    small = dot(a_high, b_low, dims) + dot(a_low, b_high, dims)
    return dot(a_high, b_high, dims) + small


def thin_dot3(a, b, dims):
    a_high, a_low = split(a)
    rows = a.shape[0]
    wide = dot(jnp.concatenate([a_high, a_low], axis=0), b[0], dims)
    return wide[:rows] + (wide[rows:] + dot(a_high, b[1], dims))


def kernel(
    leaf_rhs, front_rhs, leaf_inv, coupling, factor, inverse, parent, rows,
    leaf_out, front_out,
    rhs_v, load_v, linv_v, coup_v, rows_v, inv0_v, inv1_v, fact_v, par_s,
    par_v, recv1, send2, part2, recv2, recv3, send4, part4, recv4, loads, kept, base_v,
    inv0_s, inv1_s, fact_s, p_s, g_s, own_s, last_s,
    in_sem, par_out, par_in, core_out, core_in, load_out, load_in,
    out1, in1, out2, in2, out3, in3, out4, in4,
):
    leaf, core = lax.axis_index("leaf"), lax.axis_index("front")
    panel = inv0_v.shape[0]
    part = recv1.shape[3]
    unit = 2 * part
    count = UNITS * unit
    width = panel // LANES
    z, y, x = leaf // 16, (leaf // 4) % 4, leaf % 4

    def near(c):
        return c + 1 - 2 * (c % 2)

    def across(c):
        return 3 - c

    peers = []
    for step in (near, across):
        sx, sy, sz = step(x), step(y), step(z)
        peers.append(
            [
                (sz if k & 4 else z) * 16 + (sy if k & 2 else y) * 4 + (sx if k & 1 else x)
                for k in range(GROUP)
            ]
        )

    def local(src, dst, place):
        return pltpu.make_async_copy(src, dst, in_sem.at[place])

    loads_in = [
        local(leaf_rhs, rhs_v, 0),
        local(leaf_inv, linv_v, 1),
        local(parent, par_s, 7),
        local(coupling, coup_v, 2),
        local(rows, rows_v, 3),
    ]
    for copy in loads_in:
        copy.start()
    load_copy = local(front_rhs, load_v, 4)
    left_part = factor.at[:, pl.ds(0, panel)]

    barrier = pltpu.get_barrier_semaphore()
    for group in peers:
        for peer in group[1:]:
            pl.semaphore_signal(barrier, inc=1, device_id=(peer, core), device_id_type=MESH)
    pl.semaphore_signal(barrier, inc=1, device_id=(leaf, 1 - core), device_id_type=MESH)

    @pl.when(core == 0)
    def _():
        local(inverse, inv0_v, 5).start()

    @pl.when(core == 1)
    def _():
        local(inverse, inv1_v, 5).start()
        local(left_part, fact_v, 6).start()

    load_copy.start()

    def remote(src, dst, out_sem, into_sem, peer, side):
        return pltpu.make_async_remote_copy(
            src_ref=src, dst_ref=dst, send_sem=out_sem, recv_sem=into_sem,
            device_id=(peer, side), device_id_type=MESH,
        )

    for copy in loads_in:
        copy.wait()
    own_parent = jnp.full((8, LANES), par_s[0, 0], jnp.int32)
    par_v[0, 0] = own_parent
    par_v[1, 0] = own_parent
    rhs = jnp.concatenate(
        [rhs_v[pl.ds(0, count, stride=2), :], rhs_v[pl.ds(1, count, stride=2), :]], axis=1
    )
    leaf_inv_parts = split(linv_v[...])
    leaf_y = thin_dot3(rhs, leaf_inv_parts, NT)
    coupling_parts = split(coup_v[...])
    update = thin_dot3(leaf_y, coupling_parts, NT)
    sublane = lax.broadcasted_iota(jnp.int32, (panel, rows_v.shape[1]), 0)
    spread_to = (sublane == rows_v[...]).astype(F32).astype(BF16)
    update_parts = jnp.concatenate(split(update), axis=0)
    message = dot(update_parts, spread_to, NT)
    message = message[:count] + message[count:]
    for u in range(UNITS):
        for s in range(2):
            first_row = u * unit + s * part
            recv1[u, s, 0] = message[first_row : first_row + part]

    pl.semaphore_wait(barrier, 2 * (GROUP - 1) + 1)

    def start(src, dst, out_sem, into_sem, group, k):
        remote(src, dst, out_sem, into_sem, peers[group][k], core).start()

    def arrived(ref, sem):
        pltpu.make_async_copy(ref, ref, sem).wait()

    def gather_start(u, s, group, blocks, out_sem, in_sems):
        for k in NEXT + (7,):
            start(blocks.at[u, s, 0], blocks.at[u, s, k], out_sem, in_sems.at[u, s, k], group, k)

    def gather_relay(u, s, group, blocks, out_sem, in_sems):
        for held, to, there in RELAYS:
            arrived(blocks.at[u, s, held], in_sems.at[u, s, held])
            start(blocks.at[u, s, held], blocks.at[u, s, there], out_sem, in_sems.at[u, s, there], group, to)

    def gather_end(u, s, blocks, in_sems):
        for k in (3, 5, 6, 7):
            arrived(blocks.at[u, s, k], in_sems.at[u, s, k])

    def reduce_start(u, s, group, blocks, parts, sums, out_sem, in_sems):
        for held, to, there in RELAYS:
            start(blocks.at[u, s, there], parts.at[u, s, held], out_sem, in_sems.at[u, s, there], group, to)
        start(blocks.at[u, s, 7], sums.at[u, s, 7], out_sem, in_sems.at[u, s, 7], group, 7)

    def reduce_relay(u, s, group, blocks, parts, sums, out_sem, in_sems):
        for held, to, there in RELAYS:
            arrived(parts.at[u, s, held], in_sems.at[u, s, there])
            blocks[u, s, held] = blocks[u, s, held] + parts[u, s, held]
            start(blocks.at[u, s, held], sums.at[u, s, held], out_sem, in_sems.at[u, s, held], group, held)

    def reduce_end(u, sums, in_sems):
        totals = []
        for s in range(2):
            for k in NEXT + (7,):
                arrived(sums.at[u, s, k], in_sems.at[u, s, k])
            total = sums[u, s, 0]
            for k in NEXT + (7,):
                total = total + sums[u, s, k]
            totals.append(total)
        return jnp.concatenate(totals, axis=0)

    for s in range(2):
        for k in range(1, GROUP):
            start(par_v.at[s, 0], par_v.at[s, k], par_out, par_in.at[s, k], s, k)
    for u in range(UNITS):
        for s in range(2):
            gather_start(u, s, s, recv1, out1, in1)

    def core_copy(src, dst, place):
        return remote(src, dst, core_out.at[place], core_in.at[place], leaf, 1 - core)

    @pl.when(core == 0)
    def _():
        core_copy(inverse, inv0_v, 0).start()

    @pl.when(core == 1)
    def _():
        core_copy(inverse, inv1_v, 1).start()
        core_copy(left_part, fact_v, 2).start()

    block = 128

    def keep(where, value, at):
        high, low = split(value)
        where[0, at, :] = high
        where[1, at, :] = low

    def spans(i):
        return pl.ds(pl.multiple_of(i * block, block), block)

    def whole(ref):
        return ref[0], ref[1]

    def by_rows(ref, at):
        return ref[0, at, :], ref[1, at, :]

    def by_columns(ref, at):
        return ref[0, :, at], ref[1, :, at]

    def over(body):
        @pl.loop(0, panel // block)
        def _(i):
            body(spans(i))

    def prepare_last():
        base_v[...] = thin_dot3(leaf_y, leaf_inv_parts, NN)
        both = split(dot3(coupling_parts, leaf_inv_parts, NN))
        last = split(dot(spread_to, both[0], NN) + dot(spread_to, both[1], NN))
        last_s[0] = last[0]
        last_s[1] = last[1]

    def square(source, halves, target):
        over(lambda at: keep(halves, source[at, :], at))
        over(lambda at: keep(target, dot3(by_columns(halves, at), whole(halves), TN), at))

    def prepare_own():
        @pl.when(core == 0)
        def _():
            local(inverse, inv0_v, 5).wait()
            square(inv0_v, inv0_s, own_s)

        @pl.when(core == 1)
        def _():
            local(inverse, inv1_v, 5).wait()
            local(left_part, fact_v, 6).wait()
            square(inv1_v, inv1_s, g_s)
            over(lambda at: keep(fact_s, fact_v[at, :], at))

    def prepare_other():
        @pl.when(core == 0)
        def _():
            core_copy(inverse, inv1_v, 1).wait_recv()
            square(inv1_v, inv1_s, g_s)

        @pl.when(core == 1)
        def _():
            core_copy(inverse, inv0_v, 0).wait_recv()
            over(lambda at: keep(inv0_s, inv0_v[at, :], at))

    def prepare_product():
        @pl.when(core == 0)
        def _():
            core_copy(left_part, fact_v, 2).wait_recv()
            over(lambda at: keep(fact_s, fact_v[at, :], at))

        over(lambda at: keep(p_s, dot3(by_rows(fact_s, at), whole(inv0_s), NN), at))

    def sums(u, s):
        marks = [par_v[s, k] for k in range(GROUP)]
        targets = peers[1 - s]
        for r in range(part // 8):
            at = pl.ds(r * 8, 8)
            for c in range(width):
                lanes = pl.ds(c * LANES, LANES)
                values = [recv1[u, s, k, at, lanes] for k in range(GROUP)]
                for j in range(GROUP):
                    total = jnp.zeros((8, LANES), F32)
                    for k in range(GROUP):
                        total = total + jnp.where(marks[k] == targets[j], values[k], 0.0)
                    if j == 0:
                        recv2[u, s, 0, at, lanes] = total
                    else:
                        send2[u, s, j, at, lanes] = total

    def picks(u, s):
        marks = [par_v[s, k] for k in range(GROUP)]
        targets = peers[1 - s]
        for r in range(part // 8):
            at = pl.ds(r * 8, 8)
            for c in range(width):
                lanes = pl.ds(c * LANES, LANES)
                values = [recv3[u, s, j, at, lanes] for j in range(GROUP)]
                for k in range(GROUP):
                    picked = jnp.zeros((8, LANES), F32)
                    for j in range(GROUP):
                        picked = jnp.where(marks[k] == targets[j], values[j], picked)
                    if k == 0:
                        recv4[u, s, 0, at, lanes] = picked
                    else:
                        send4[u, s, k, at, lanes] = picked

    def relay_update(u):
        for s in range(2):
            gather_relay(u, s, s, recv1, out1, in1)

    def sum_updates(u):
        if u == 0:
            for s in range(2):
                for k in range(1, GROUP):
                    arrived(par_v.at[s, k], par_in.at[s, k])
        for s in range(2):
            gather_end(u, s, recv1, in1)
            sums(u, s)
            reduce_start(u, s, 1 - s, send2, part2, recv2, out2, in2)

    def relay_sums(u):
        for s in range(2):
            reduce_relay(u, s, 1 - s, send2, part2, recv2, out2, in2)

    def swap(u):
        return remote(loads.at[0, u], loads.at[1, u], load_out.at[u], load_in.at[u], leaf, 1 - core)

    def swap_load(u):
        if u == 0:
            load_copy.wait()
        total = reduce_end(u, recv2, in2)
        given = jnp.concatenate(
            [load_v[pl.ds(u * unit * width + c, unit, stride=width), :] for c in range(width)], axis=1
        )
        load = given - total
        loads[0, u] = load
        swap(u).start()

        @pl.when(core == 0)
        def _():
            kept[0, u] = thin_dot3(load, whole(own_s), NN)
            kept[1, u] = thin_dot3(load, whole(p_s), NT)

    def solve(u):
        swap(u).wait_recv()

        def give(solution):
            for s in range(2):
                recv3[u, s, 0] = solution[s * part : (s + 1) * part]
            for c in range(width):
                front_out[pl.ds(u * unit * width + c, unit, stride=width), :] = solution[:, c * LANES : (c + 1) * LANES]

        @pl.when(core == 0)
        def _():
            later = thin_dot3(loads[1, u] - kept[1, u], whole(g_s), NN)
            give(kept[0, u] - thin_dot3(later, whole(p_s), NN))

        @pl.when(core == 1)
        def _():
            pending = loads[0, u] - thin_dot3(loads[1, u], whole(p_s), NT)
            give(thin_dot3(pending, whole(g_s), NN))

        for s in range(2):
            gather_start(u, s, 1 - s, recv3, out3, in3)

    def relay_solution(u):
        for s in range(2):
            gather_relay(u, s, 1 - s, recv3, out3, in3)

    def pick_panels(u):
        for s in range(2):
            gather_end(u, s, recv3, in3)
            picks(u, s)
            reduce_start(u, s, s, send4, part4, recv4, out4, in4)

    def relay_panels(u):
        for s in range(2):
            reduce_relay(u, s, s, send4, part4, recv4, out4, in4)

    def finish(u):
        total = reduce_end(u, recv4, in4)
        result = base_v[pl.ds(u * unit, unit), :] - thin_dot3(total, whole(last_s), NN)
        for c in range(2):
            leaf_out[pl.ds(u * unit * 2 + c, unit, stride=2), :] = result[:, c * LANES : (c + 1) * LANES]

    plan = [(0.0, prepare_last), (0.5, prepare_own), (3.5, prepare_other), (4.3, prepare_product)]
    stages = (
        (2.1, 0.4, relay_update), (4.5, 0.9, sum_updates), (6.8, 0.9, relay_sums), (9.2, 0.9, swap_load),
        (10.4, 0.9, solve), (12.5, 0.9, relay_solution), (14.8, 0.9, pick_panels), (17.0, 0.9, relay_panels),
        (19.4, 0.9, finish),
    )
    for begin, step, stage in stages:
        for u in range(UNITS):
            plan.append((begin + step * u * 4 / UNITS, lambda stage=stage, u=u: stage(u)))
    for _, task in sorted(plan, key=lambda entry: entry[0]):
        task()

    for blocks, sem in ((recv1, out1), (recv2, out2), (recv3, out3), (recv4, out4)):
        seven = blocks.at[:, :, pl.ds(1, GROUP - 1)]
        arrived(seven, sem)
    arrived(par_v.at[:, pl.ds(1, GROUP - 1)], par_out)
    for u in range(UNITS):
        swap(u).wait_send()

    @pl.when(core == 0)
    def _():
        core_copy(inverse, inv0_v, 0).wait_send()

    @pl.when(core == 1)
    def _():
        core_copy(inverse, inv1_v, 1).wait_send()
        core_copy(left_part, fact_v, 2).wait_send()


def on_device(leaf_rhs, front_rhs, leaf_inverse, coupling, front_factor, front_inverse, parent, rows):
    batches, each = leaf_rhs.shape[:2]
    snode, panel = leaf_rhs.shape[4], front_rhs.shape[3]
    count, crows = batches * each, rows.shape[2]
    part = count // (2 * UNITS)
    slots = pltpu.VMEM((UNITS, 2, GROUP, part, panel), F32)
    square = pltpu.VMEM((panel, panel), F32)
    pair = pltpu.VMEM((2, panel, panel), BF16)
    halves = pltpu.VMEM((2, UNITS, 2 * part, panel), F32)
    dma = pltpu.SemaphoreType.DMA
    hbm, vmem = pl.BlockSpec(memory_space=pltpu.HBM), pl.BlockSpec(memory_space=pltpu.VMEM)
    leaf_x, front_x = pl.pallas_call(
        kernel,
        out_shape=(
            jax.ShapeDtypeStruct((count * snode // LANES, LANES), F32),
            jax.ShapeDtypeStruct((count * panel // LANES, LANES), F32),
        ),
        in_specs=[hbm] * 8,
        out_specs=(vmem, vmem),
        scratch_shapes=[
            pltpu.VMEM((count * snode // LANES, LANES), F32),
            pltpu.VMEM((count * panel // LANES, LANES), F32),
            pltpu.VMEM((snode, snode), F32),
            pltpu.VMEM((crows, snode), F32),
            pltpu.VMEM((1, crows), jnp.int32),
            square, square, square,
            pltpu.SMEM((1, 1), jnp.int32),
            pltpu.VMEM((2, GROUP, 8, LANES), jnp.int32),
            slots, slots, slots, slots, slots, slots, slots, slots,
            halves, halves,
            pltpu.VMEM((count, snode), F32),
            pair, pair, pair, pair, pair, pair,
            pltpu.VMEM((2, panel, snode), BF16),
            dma((8,)), dma, dma((2, GROUP)), dma((3,)), dma((3,)), dma((UNITS,)), dma((UNITS,)),
        ] + [dma, dma((UNITS, 2, GROUP))] * 4,
        compiler_params=pltpu.CompilerParams(
            collective_id=0, has_side_effects=True, vmem_limit_bytes=67043328
        ),
    )(
        leaf_rhs.reshape(count * snode // LANES, LANES),
        front_rhs.reshape(count * panel // LANES, LANES),
        leaf_inverse[0, 0],
        coupling[0, 0],
        front_factor[0],
        front_inverse[0],
        parent,
        rows[0],
    )
    return (
        leaf_x.reshape(batches, each, 1, 1, snode),
        front_x.reshape(batches, each, 1, panel),
    )


def solution(mesh):
    placed = (
        P(None, None, "leaf", "front", None),
        P(None, None, "leaf", "front"),
        P("leaf", "front", None, None),
        P("leaf", "front", None, None),
        P("leaf", "front", None),
        P("leaf", "front", None),
        P("leaf", "front"),
        P("leaf", "front", None),
    )
    return jax.shard_map(
        on_device,
        mesh=mesh,
        in_specs=placed,
        out_specs=(P(None, None, "leaf", "front", None), P(None, None, "leaf", "front")),
        check_vma=False,
    )
```

time: 59.3 us -> 53.2 us (0.90)
  local copies, waits for them, and re-layouts: 6.87 us -> 3.04 us
  Pallas kernels: 50.5 us -> 48.7 us
    unnamed x14 -> x2, local copies, waits for them, and re-layouts: 6.87 us -> 3.04 us
    pallas_call x1, Pallas kernels: 50.5 us -> 48.7 us  [on_device(): pl.pallas_call(kernel, out_shape=(jax.ShapeDtypeStruct((count * snode //...]
where the time goes in v2:
time: 53.2 us; the launch traced here: 53 us
  Pallas kernels  48.7 us (92%)
  local copies, waits for them, and re-layouts  3.04 us (6%)
  between operations  1.29 us (2%)
    pallas_call x1, Pallas kernels, on_device(): pl.pallas_call(kernel, out_shape=(jax.ShapeDtypeStruct((count * snode //...  48.7 us
    unnamed x2, local copies, waits for them, and re-layouts  3.04 us

profile of v2, /device:TPU:0, one launch (start us, length us, event | category | flops | bytes accessed | tf_op | source)
XLA Modules:
  0.0 53.0 jit_solution(16547574522108579897)
XLA Ops:
  1.3 48.7 %shard_map.95 = (f32[128,128]{1,0:T(8,128)}, f32[256,128]{1,0:T(8,128)}) custom-call(f32[128,128]{1,0:T(8,128)} %bitcast.15, f32[256,128]{1,0:T(8,128)} %bitcast.13, f32[256,256]{1,0:T(8,128)} %bitcast.12, f32[384,256]{1,0:T(8,128)} %bitcast.11, f32[512,1024]{1,0:T(8,128)} %bitcast.9, f32[512,512]{1,0:T(8,128)} %bitcast.10, s32[1,1]{1,0:T(1,128)S(6)} %copy.14.parent, ...), custom_call_target="tpu_custom_call" | custom-call | tf_op jit(solution)/shard_map/pallas_call | solution.py:417
  50.0 1.5 %copy.15 = f32[2,32,1,1,256]{4,3,2,1,0:T(1,128)} copy(f32[2,32,1,1,256]{4,3,2,1,0:T(1,128)} %bitcast.16) | data formatting | bytes 131072
  51.5 1.6 %copy.16 = f32[2,32,1,512]{3,2,1,0:T(1,128)} copy(f32[2,32,1,512]{3,2,1,0:T(1,128)} %bitcast.14) | data formatting | bytes 262144

commit v3 on v2

--- a/solution.py
+++ b/solution.py
@@ -12,9 +12,8 @@
 F32, BF16 = jnp.float32, jnp.bfloat16
 LANES = 128
 GROUP = 8
-UNITS = 4
-NEXT = (1, 2, 4)
-RELAYS = ((2, 1, 3), (4, 2, 6), (1, 4, 5))
+UNITS = 2
+FAR_FIRST = (7, 3, 5, 6, 1, 2, 4)
 
 
 def split(value):
@@ -40,10 +39,10 @@
 
 
 def kernel(
-    leaf_rhs, front_rhs, leaf_inv, coupling, factor, inverse, parent, rows,
+    leaf_rhs, front_rhs, leaf_inv, coupling, factor, inverse, rows, parent,
     leaf_out, front_out,
-    rhs_v, load_v, linv_v, coup_v, rows_v, inv0_v, inv1_v, fact_v, par_s,
-    par_v, recv1, send2, part2, recv2, recv3, send4, part4, recv4, loads, kept, base_v,
+    rhs_v, load_v, linv_v, coup_v, rows_v, inv0_v, inv1_v, fact_v,
+    par_v, recv1, send2, recv2, recv3, send4, recv4, loads, kept, base_v,
     inv0_s, inv1_s, fact_s, p_s, g_s, own_s, last_s,
     in_sem, par_out, par_in, core_out, core_in, load_out, load_in,
     out1, in1, out2, in2, out3, in3, out4, in4,
@@ -78,7 +77,6 @@
     loads_in = [
         local(leaf_rhs, rhs_v, 0),
         local(leaf_inv, linv_v, 1),
-        local(parent, par_s, 7),
         local(coupling, coup_v, 2),
         local(rows, rows_v, 3),
     ]
@@ -110,11 +108,19 @@
             device_id=(peer, side), device_id_type=MESH,
         )
 
+    def start(src, dst, out_sem, into_sem, group, k):
+        remote(src, dst, out_sem, into_sem, peers[group][k], core).start()
+
+    own_parent = jnp.full((8, LANES), parent[0, 0], jnp.int32)
+    par_v[0, 0] = own_parent
+    par_v[1, 0] = own_parent
+    pl.semaphore_wait(barrier, 2 * (GROUP - 1) + 1)
+    for s in range(2):
+        for k in FAR_FIRST:
+            start(par_v.at[s, 0], par_v.at[s, k], par_out, par_in.at[s, k], s, k)
+
     for copy in loads_in:
         copy.wait()
-    own_parent = jnp.full((8, LANES), par_s[0, 0], jnp.int32)
-    par_v[0, 0] = own_parent
-    par_v[1, 0] = own_parent
     rhs = jnp.concatenate(
         [rhs_v[pl.ds(0, count, stride=2), :], rhs_v[pl.ds(1, count, stride=2), :]], axis=1
     )
@@ -132,52 +138,32 @@
             first_row = u * unit + s * part
             recv1[u, s, 0] = message[first_row : first_row + part]
 
-    pl.semaphore_wait(barrier, 2 * (GROUP - 1) + 1)
-
-    def start(src, dst, out_sem, into_sem, group, k):
-        remote(src, dst, out_sem, into_sem, peers[group][k], core).start()
-
     def arrived(ref, sem):
         pltpu.make_async_copy(ref, ref, sem).wait()
 
     def gather_start(u, s, group, blocks, out_sem, in_sems):
-        for k in NEXT + (7,):
+        for k in FAR_FIRST:
             start(blocks.at[u, s, 0], blocks.at[u, s, k], out_sem, in_sems.at[u, s, k], group, k)
 
-    def gather_relay(u, s, group, blocks, out_sem, in_sems):
-        for held, to, there in RELAYS:
-            arrived(blocks.at[u, s, held], in_sems.at[u, s, held])
-            start(blocks.at[u, s, held], blocks.at[u, s, there], out_sem, in_sems.at[u, s, there], group, to)
-
     def gather_end(u, s, blocks, in_sems):
-        for k in (3, 5, 6, 7):
+        for k in FAR_FIRST:
             arrived(blocks.at[u, s, k], in_sems.at[u, s, k])
 
-    def reduce_start(u, s, group, blocks, parts, sums, out_sem, in_sems):
-        for held, to, there in RELAYS:
-            start(blocks.at[u, s, there], parts.at[u, s, held], out_sem, in_sems.at[u, s, there], group, to)
-        start(blocks.at[u, s, 7], sums.at[u, s, 7], out_sem, in_sems.at[u, s, 7], group, 7)
-
-    def reduce_relay(u, s, group, blocks, parts, sums, out_sem, in_sems):
-        for held, to, there in RELAYS:
-            arrived(parts.at[u, s, held], in_sems.at[u, s, there])
-            blocks[u, s, held] = blocks[u, s, held] + parts[u, s, held]
-            start(blocks.at[u, s, held], sums.at[u, s, held], out_sem, in_sems.at[u, s, held], group, held)
+    def reduce_start(u, s, group, blocks, sums, out_sem, in_sems):
+        for k in FAR_FIRST:
+            start(blocks.at[u, s, k], sums.at[u, s, k], out_sem, in_sems.at[u, s, k], group, k)
 
     def reduce_end(u, sums, in_sems):
         totals = []
         for s in range(2):
-            for k in NEXT + (7,):
+            for k in FAR_FIRST:
                 arrived(sums.at[u, s, k], in_sems.at[u, s, k])
             total = sums[u, s, 0]
-            for k in NEXT + (7,):
+            for k in range(1, GROUP):
                 total = total + sums[u, s, k]
             totals.append(total)
         return jnp.concatenate(totals, axis=0)
 
-    for s in range(2):
-        for k in range(1, GROUP):
-            start(par_v.at[s, 0], par_v.at[s, k], par_out, par_in.at[s, k], s, k)
     for u in range(UNITS):
         for s in range(2):
             gather_start(u, s, s, recv1, out1, in1)
@@ -295,10 +281,6 @@
                     else:
                         send4[u, s, k, at, lanes] = picked
 
-    def relay_update(u):
-        for s in range(2):
-            gather_relay(u, s, s, recv1, out1, in1)
-
     def sum_updates(u):
         if u == 0:
             for s in range(2):
@@ -307,11 +289,7 @@
         for s in range(2):
             gather_end(u, s, recv1, in1)
             sums(u, s)
-            reduce_start(u, s, 1 - s, send2, part2, recv2, out2, in2)
-
-    def relay_sums(u):
-        for s in range(2):
-            reduce_relay(u, s, 1 - s, send2, part2, recv2, out2, in2)
+            reduce_start(u, s, 1 - s, send2, recv2, out2, in2)
 
     def swap(u):
         return remote(loads.at[0, u], loads.at[1, u], load_out.at[u], load_in.at[u], leaf, 1 - core)
@@ -354,19 +332,11 @@
         for s in range(2):
             gather_start(u, s, 1 - s, recv3, out3, in3)
 
-    def relay_solution(u):
-        for s in range(2):
-            gather_relay(u, s, 1 - s, recv3, out3, in3)
-
     def pick_panels(u):
         for s in range(2):
             gather_end(u, s, recv3, in3)
             picks(u, s)
-            reduce_start(u, s, s, send4, part4, recv4, out4, in4)
-
-    def relay_panels(u):
-        for s in range(2):
-            reduce_relay(u, s, s, send4, part4, recv4, out4, in4)
+            reduce_start(u, s, s, send4, recv4, out4, in4)
 
     def finish(u):
         total = reduce_end(u, recv4, in4)
@@ -374,11 +344,9 @@
         for c in range(2):
             leaf_out[pl.ds(u * unit * 2 + c, unit, stride=2), :] = result[:, c * LANES : (c + 1) * LANES]
 
-    plan = [(0.0, prepare_last), (0.5, prepare_own), (3.5, prepare_other), (4.3, prepare_product)]
+    plan = [(0.0, prepare_last), (0.5, prepare_own), (3.5, prepare_other), (5.9, prepare_product)]
     stages = (
-        (2.1, 0.4, relay_update), (4.5, 0.9, sum_updates), (6.8, 0.9, relay_sums), (9.2, 0.9, swap_load),
-        (10.4, 0.9, solve), (12.5, 0.9, relay_solution), (14.8, 0.9, pick_panels), (17.0, 0.9, relay_panels),
-        (19.4, 0.9, finish),
+        (4.7, 1.2, sum_updates), (9.5, 1.2, swap_load), (10.7, 1.2, solve), (15.8, 1.2, pick_panels), (20.8, 1.2, finish),
     )
     for begin, step, stage in stages:
         for u in range(UNITS):
@@ -417,10 +385,10 @@
     leaf_x, front_x = pl.pallas_call(
         kernel,
         out_shape=(
-            jax.ShapeDtypeStruct((count * snode // LANES, LANES), F32),
-            jax.ShapeDtypeStruct((count * panel // LANES, LANES), F32),
+            pltpu.VMEM((count * snode // LANES, LANES), F32),
+            pltpu.VMEM((count * panel // LANES, LANES), F32),
         ),
-        in_specs=[hbm] * 8,
+        in_specs=[hbm] * 7 + [pl.BlockSpec(memory_space=pltpu.SMEM)],
         out_specs=(vmem, vmem),
         scratch_shapes=[
             pltpu.VMEM((count * snode // LANES, LANES), F32),
@@ -429,9 +397,8 @@
             pltpu.VMEM((crows, snode), F32),
             pltpu.VMEM((1, crows), jnp.int32),
             square, square, square,
-            pltpu.SMEM((1, 1), jnp.int32),
             pltpu.VMEM((2, GROUP, 8, LANES), jnp.int32),
-            slots, slots, slots, slots, slots, slots, slots, slots,
+            slots, slots, slots, slots, slots, slots,
             halves, halves,
             pltpu.VMEM((count, snode), F32),
             pair, pair, pair, pair, pair, pair,
@@ -439,17 +406,22 @@
             dma((8,)), dma, dma((2, GROUP)), dma((3,)), dma((3,)), dma((UNITS,)), dma((UNITS,)),
         ] + [dma, dma((UNITS, 2, GROUP))] * 4,
         compiler_params=pltpu.CompilerParams(
-            collective_id=0, has_side_effects=True, vmem_limit_bytes=67043328
+            collective_id=0, has_side_effects=True, vmem_limit_bytes=60 << 20
         ),
     )(
-        leaf_rhs.reshape(count * snode // LANES, LANES),
-        front_rhs.reshape(count * panel // LANES, LANES),
-        leaf_inverse[0, 0],
-        coupling[0, 0],
-        front_factor[0],
-        front_inverse[0],
+        *(
+            pltpu.with_memory_space_constraint(value, pltpu.HBM)
+            for value in (
+                leaf_rhs.reshape(count * snode // LANES, LANES),
+                front_rhs.reshape(count * panel // LANES, LANES),
+                leaf_inverse[0, 0],
+                coupling[0, 0],
+                front_factor[0],
+                front_inverse[0],
+                rows[0],
+            )
+        ),
         parent,
-        rows[0],
     )
     return (
         leaf_x.reshape(batches, each, 1, 1, snode),

time: 53.2 us -> 42.7 us (0.80)
  Pallas kernels: 48.7 us -> 40 us
  local copies, waits for them, and re-layouts: 3.04 us -> 1.29 us
    pallas_call x1, Pallas kernels: 48.7 us -> 40 us  [on_device(): pl.pallas_call(kernel, out_shape=(pltpu.VMEM((count * snode // LANES, LAN...]
    unnamed x2, local copies, waits for them, and re-layouts: 3.04 us -> 1.29 us
where the time goes in v3:
time: 42.7 us; the launch traced here: 42.6 us
  Pallas kernels  40 us (94%)
  local copies, waits for them, and re-layouts  1.29 us (3%)
  between operations  1.29 us (3%)
    pallas_call x1, Pallas kernels, on_device(): pl.pallas_call(kernel, out_shape=(pltpu.VMEM((count * snode // LANES, LAN...  40 us
    unnamed x2, local copies, waits for them, and re-layouts  1.29 us

profile of v3, /device:TPU:0, one launch (start us, length us, event | category | flops | bytes accessed | tf_op | source)
XLA Modules:
  0.0 42.6 jit_solution(12778532245806295605)
XLA Ops:
  1.3 40.0 %shard_map.95 = (f32[128,128]{1,0:T(8,128)S(1)}, f32[256,128]{1,0:T(8,128)S(1)}) custom-call(f32[128,128]{1,0:T(8,128)} %bitcast.16, f32[256,128]{1,0:T(8,128)} %bitcast.15, f32[256,256]{1,0:T(8,128)} %bitcast.14, f32[384,256]{1,0:T(8,128)} %bitcast.13, f32[512,1024]{1,0:T(8,128)} %bitcast.11, f32[512,512]{1,0:T(8,128)} %bitcast.12, s32[1,384]{1,0:T(1,128)} %bitcast.17, ...), custom_call_target="tpu_custom_call" | custom-call | tf_op jit(solution)/shard_map/pallas_call | solution.py:385
  41.3 0.6 %copy.14 = f32[2,32,1,1,256]{4,3,2,1,0:T(1,128)} copy(f32[2,32,1,1,256]{4,3,2,1,0:T(1,128)S(1)} %bitcast.10) | data formatting | bytes 131072
  41.9 0.7 %copy.15 = f32[2,32,1,512]{3,2,1,0:T(1,128)} copy(f32[2,32,1,512]{3,2,1,0:T(1,128)S(1)} %bitcast.9) | data formatting | bytes 262144

commit v4 on v3

--- a/solution.py
+++ b/solution.py
@@ -13,6 +13,7 @@
 LANES = 128
 GROUP = 8
 UNITS = 2
+FIRST, SECOND = (0, 1, 1), (1, 0, 0)
 FAR_FIRST = (7, 3, 5, 6, 1, 2, 4)
 
 
@@ -43,7 +44,7 @@
     leaf_out, front_out,
     rhs_v, load_v, linv_v, coup_v, rows_v, inv0_v, inv1_v, fact_v,
     par_v, recv1, send2, recv2, recv3, send4, recv4, loads, kept, base_v,
-    inv0_s, inv1_s, fact_s, p_s, g_s, own_s, last_s,
+    inv0_s, inv1_s, fact_s, p_s, g_s, own_s, last_s, onehot_s,
     in_sem, par_out, par_in, core_out, core_in, load_out, load_in,
     out1, in1, out2, in2, out3, in3, out4, in4,
 ):
@@ -62,8 +63,8 @@
         return 3 - c
 
     peers = []
-    for step in (near, across):
-        sx, sy, sz = step(x), step(y), step(z)
+    for steps in (FIRST, SECOND):
+        sz, sy, sx = (across(c) if far else near(c) for far, c in zip(steps, (z, y, x)))
         peers.append(
             [
                 (sz if k & 4 else z) * 16 + (sy if k & 2 else y) * 4 + (sx if k & 1 else x)
@@ -75,21 +76,21 @@
         return pltpu.make_async_copy(src, dst, in_sem.at[place])
 
     loads_in = [
+        local(rows, rows_v, 3),
         local(leaf_rhs, rhs_v, 0),
         local(leaf_inv, linv_v, 1),
         local(coupling, coup_v, 2),
-        local(rows, rows_v, 3),
     ]
+    load_copy = local(front_rhs, load_v, 4)
+    left_part = factor.at[:, pl.ds(0, panel)]
+
+    barrier = pltpu.get_barrier_semaphore()
+    for k in FAR_FIRST:
+        for group in peers:
+            pl.semaphore_signal(barrier, inc=1, device_id=(group[k], core), device_id_type=MESH)
+    pl.semaphore_signal(barrier, inc=1, device_id=(leaf, 1 - core), device_id_type=MESH)
     for copy in loads_in:
         copy.start()
-    load_copy = local(front_rhs, load_v, 4)
-    left_part = factor.at[:, pl.ds(0, panel)]
-
-    barrier = pltpu.get_barrier_semaphore()
-    for group in peers:
-        for peer in group[1:]:
-            pl.semaphore_signal(barrier, inc=1, device_id=(peer, core), device_id_type=MESH)
-    pl.semaphore_signal(barrier, inc=1, device_id=(leaf, 1 - core), device_id_type=MESH)
 
     @pl.when(core == 0)
     def _():
@@ -114,30 +115,34 @@
     own_parent = jnp.full((8, LANES), parent[0, 0], jnp.int32)
     par_v[0, 0] = own_parent
     par_v[1, 0] = own_parent
+
+    loads_in[0].wait()
+    sublane = lax.broadcasted_iota(jnp.int32, (panel, rows_v.shape[1]), 0)
+    onehot_s[...] = (sublane == rows_v[...]).astype(F32).astype(BF16)
+    loads_in[1].wait()
+    rhs = jnp.concatenate(
+        [rhs_v[pl.ds(0, count, stride=2), :], rhs_v[pl.ds(1, count, stride=2), :]], axis=1
+    )
+    loads_in[2].wait()
+    leaf_inv_parts = split(linv_v[...])
+    leaf_y = thin_dot3(rhs, leaf_inv_parts, NT)
+    loads_in[3].wait()
+    coupling_parts = split(coup_v[...])
+    update = thin_dot3(leaf_y, coupling_parts, NT)
+    spread_to = onehot_s[...]
+    update_parts = jnp.concatenate(split(update), axis=0)
+    message = dot(update_parts, spread_to, NT)
+    message = message[:count] + message[count:]
+    for u in range(UNITS):
+        for s in range(2):
+            first_row = u * unit + s * part
+            recv1[u, s, 0] = message[first_row : first_row + part]
+
     pl.semaphore_wait(barrier, 2 * (GROUP - 1) + 1)
     for s in range(2):
         for k in FAR_FIRST:
             start(par_v.at[s, 0], par_v.at[s, k], par_out, par_in.at[s, k], s, k)
 
-    for copy in loads_in:
-        copy.wait()
-    rhs = jnp.concatenate(
-        [rhs_v[pl.ds(0, count, stride=2), :], rhs_v[pl.ds(1, count, stride=2), :]], axis=1
-    )
-    leaf_inv_parts = split(linv_v[...])
-    leaf_y = thin_dot3(rhs, leaf_inv_parts, NT)
-    coupling_parts = split(coup_v[...])
-    update = thin_dot3(leaf_y, coupling_parts, NT)
-    sublane = lax.broadcasted_iota(jnp.int32, (panel, rows_v.shape[1]), 0)
-    spread_to = (sublane == rows_v[...]).astype(F32).astype(BF16)
-    update_parts = jnp.concatenate(split(update), axis=0)
-    message = dot(update_parts, spread_to, NT)
-    message = message[:count] + message[count:]
-    for u in range(UNITS):
-        for s in range(2):
-            first_row = u * unit + s * part
-            recv1[u, s, 0] = message[first_row : first_row + part]
-
     def arrived(ref, sem):
         pltpu.make_async_copy(ref, ref, sem).wait()
 
@@ -149,9 +154,11 @@
         for k in FAR_FIRST:
             arrived(blocks.at[u, s, k], in_sems.at[u, s, k])
 
-    def reduce_start(u, s, group, blocks, sums, out_sem, in_sems):
-        for k in FAR_FIRST:
+    def reduce_send(u, s, group, blocks, sums, out_sem, in_sems):
+        def send(k):
             start(blocks.at[u, s, k], sums.at[u, s, k], out_sem, in_sems.at[u, s, k], group, k)
+
+        return send
 
     def reduce_end(u, sums, in_sems):
         totals = []
@@ -247,39 +254,46 @@
 
         over(lambda at: keep(p_s, dot3(by_rows(fact_s, at), whole(inv0_s), NN), at))
 
-    def sums(u, s):
+    def each_slot(own, others, work, send):
+        ready = None
+        for k in FAR_FIRST:
+            work(k, others)
+            if ready is not None:
+                send(ready)
+            ready = k
+        work(0, own)
+        send(ready)
+
+    def tiles():
+        for r in range(part // 8):
+            for c in range(width):
+                yield pl.ds(r * 8, 8), pl.ds(c * LANES, LANES)
+
+    def sums(u, s, send):
         marks = [par_v[s, k] for k in range(GROUP)]
-        targets = peers[1 - s]
-        for r in range(part // 8):
-            at = pl.ds(r * 8, 8)
-            for c in range(width):
-                lanes = pl.ds(c * LANES, LANES)
-                values = [recv1[u, s, k, at, lanes] for k in range(GROUP)]
+
+        def work(j, into):
+            chosen = [mark == peers[1 - s][j] for mark in marks]
+            for at, lanes in tiles():
+                terms = [jnp.where(chosen[k], recv1[u, s, k, at, lanes], 0.0) for k in range(GROUP)]
+                while len(terms) > 1:
+                    terms = [a + b for a, b in zip(terms[::2], terms[1::2])]
+                into[u, s, j, at, lanes] = terms[0]
+
+        each_slot(recv2, send2, work, send)
+
+    def picks(u, s, send):
+        marks = [par_v[s, k] for k in range(GROUP)]
+
+        def work(k, into):
+            chosen = [marks[k] == peers[1 - s][j] for j in range(GROUP)]
+            for at, lanes in tiles():
+                picked = jnp.zeros((8, LANES), F32)
                 for j in range(GROUP):
-                    total = jnp.zeros((8, LANES), F32)
-                    for k in range(GROUP):
-                        total = total + jnp.where(marks[k] == targets[j], values[k], 0.0)
-                    if j == 0:
-                        recv2[u, s, 0, at, lanes] = total
-                    else:
-                        send2[u, s, j, at, lanes] = total
-
-    def picks(u, s):
-        marks = [par_v[s, k] for k in range(GROUP)]
-        targets = peers[1 - s]
-        for r in range(part // 8):
-            at = pl.ds(r * 8, 8)
-            for c in range(width):
-                lanes = pl.ds(c * LANES, LANES)
-                values = [recv3[u, s, j, at, lanes] for j in range(GROUP)]
-                for k in range(GROUP):
-                    picked = jnp.zeros((8, LANES), F32)
-                    for j in range(GROUP):
-                        picked = jnp.where(marks[k] == targets[j], values[j], picked)
-                    if k == 0:
-                        recv4[u, s, 0, at, lanes] = picked
-                    else:
-                        send4[u, s, k, at, lanes] = picked
+                    picked = jnp.where(chosen[j], recv3[u, s, j, at, lanes], picked)
+                into[u, s, k, at, lanes] = picked
+
+        each_slot(recv4, send4, work, send)
 
     def sum_updates(u):
         if u == 0:
@@ -288,8 +302,7 @@
                     arrived(par_v.at[s, k], par_in.at[s, k])
         for s in range(2):
             gather_end(u, s, recv1, in1)
-            sums(u, s)
-            reduce_start(u, s, 1 - s, send2, recv2, out2, in2)
+            sums(u, s, reduce_send(u, s, 1 - s, send2, recv2, out2, in2))
 
     def swap(u):
         return remote(loads.at[0, u], loads.at[1, u], load_out.at[u], load_in.at[u], leaf, 1 - core)
@@ -335,8 +348,7 @@
     def pick_panels(u):
         for s in range(2):
             gather_end(u, s, recv3, in3)
-            picks(u, s)
-            reduce_start(u, s, s, send4, recv4, out4, in4)
+            picks(u, s, reduce_send(u, s, s, send4, recv4, out4, in4))
 
     def finish(u):
         total = reduce_end(u, recv4, in4)
@@ -369,6 +381,17 @@
     def _():
         core_copy(inverse, inv1_v, 1).wait_send()
         core_copy(left_part, fact_v, 2).wait_send()
+
+
+def put_out(leaf_in, front_in, leaf_out, front_out, sem):
+    copies = [
+        pltpu.make_async_copy(leaf_in, leaf_out, sem.at[0]),
+        pltpu.make_async_copy(front_in, front_out, sem.at[1]),
+    ]
+    for copy in copies:
+        copy.start()
+    for copy in copies:
+        copy.wait()
 
 
 def on_device(leaf_rhs, front_rhs, leaf_inverse, coupling, front_factor, front_inverse, parent, rows):
@@ -403,6 +426,7 @@
             pltpu.VMEM((count, snode), F32),
             pair, pair, pair, pair, pair, pair,
             pltpu.VMEM((2, panel, snode), BF16),
+            pltpu.VMEM((panel, crows), BF16),
             dma((8,)), dma, dma((2, GROUP)), dma((3,)), dma((3,)), dma((UNITS,)), dma((UNITS,)),
         ] + [dma, dma((UNITS, 2, GROUP))] * 4,
         compiler_params=pltpu.CompilerParams(
@@ -423,6 +447,16 @@
         ),
         parent,
     )
+    leaf_x, front_x = pl.pallas_call(
+        put_out,
+        out_shape=(
+            pltpu.HBM((count * snode // LANES, LANES), F32),
+            pltpu.HBM((count * panel // LANES, LANES), F32),
+        ),
+        in_specs=[vmem] * 2,
+        out_specs=(hbm, hbm),
+        scratch_shapes=[dma((2,))],
+    )(*(pltpu.with_memory_space_constraint(value, pltpu.VMEM) for value in (leaf_x, front_x)))
     return (
         leaf_x.reshape(batches, each, 1, 1, snode),
         front_x.reshape(batches, each, 1, panel),

time: 42.7 us -> 40.6 us (0.951)
  the two profiles are of different devices: /device:TPU:0 before, /device:TPU:1 now
where the time goes in v4:
time: 40.6 us; the launch traced here: 40.4 us
  Pallas kernels  39.1 us (96%)
  between operations  1.29 us (3%)
    pallas_call x1, Pallas kernels, on_device(): pl.pallas_call(kernel, out_shape=(pltpu.VMEM((count * snode // LANES, LAN...  38.5 us

profile of v4, /device:TPU:1, one launch (start us, length us, event | category | flops | bytes accessed | tf_op | source)
XLA Modules:
  0.0 40.4 jit_solution(11720326767671813508)
XLA Ops:
  1.3 38.5 %shard_map.95 = (f32[128,128]{1,0:T(8,128)S(1)}, f32[256,128]{1,0:T(8,128)S(1)}) custom-call(f32[128,128]{1,0:T(8,128)} %bitcast.14, f32[256,128]{1,0:T(8,128)} %bitcast.13, f32[256,256]{1,0:T(8,128)} %bitcast.12, f32[384,256]{1,0:T(8,128)} %bitcast.11, f32[512,1024]{1,0:T(8,128)} %bitcast.9, f32[512,512]{1,0:T(8,128)} %bitcast.10, s32[1,384]{1,0:T(1,128)} %bitcast.15, ...), custom_call_target="tpu_custom_call" | custom-call | tf_op jit(solution)/shard_map/pallas_call | solution.py:408
  39.7 0.7 %shard_map.96 = (f32[128,128]{1,0:T(8,128)}, f32[256,128]{1,0:T(8,128)}) custom-call(f32[128,128]{1,0:T(8,128)S(1)} %get-tuple-element.6.leaf_in, f32[256,128]{1,0:T(8,128)S(1)} %get-tuple-element.7.front_in), custom_call_target="tpu_custom_call" | custom-call | tf_op jit(solution)/shard_map/pallas_call | solution.py:450

commit v5 on v4

--- a/solution.py
+++ b/solution.py
@@ -44,7 +44,7 @@
     leaf_out, front_out,
     rhs_v, load_v, linv_v, coup_v, rows_v, inv0_v, inv1_v, fact_v,
     par_v, recv1, send2, recv2, recv3, send4, recv4, loads, kept, base_v,
-    inv0_s, inv1_s, fact_s, p_s, g_s, own_s, last_s, onehot_s,
+    inv0_s, inv1_s, fact_s, p_s, g_s, own_s, other_s, last_s, onehot_s,
     in_sem, par_out, par_in, core_out, core_in, load_out, load_in,
     out1, in1, out2, in2, out3, in3, out4, in4,
 ):
@@ -112,7 +112,7 @@
     def start(src, dst, out_sem, into_sem, group, k):
         remote(src, dst, out_sem, into_sem, peers[group][k], core).start()
 
-    own_parent = jnp.full((8, LANES), parent[0, 0], jnp.int32)
+    own_parent = jnp.full((1, LANES), parent[0, 0], jnp.int32)
     par_v[0, 0] = own_parent
     par_v[1, 0] = own_parent
 
@@ -232,7 +232,7 @@
         def _():
             local(inverse, inv1_v, 5).wait()
             local(left_part, fact_v, 6).wait()
-            square(inv1_v, inv1_s, g_s)
+            square(inv1_v, inv1_s, own_s)
             over(lambda at: keep(fact_s, fact_v[at, :], at))
 
     def prepare_other():
@@ -253,6 +253,22 @@
             over(lambda at: keep(fact_s, fact_v[at, :], at))
 
         over(lambda at: keep(p_s, dot3(by_rows(fact_s, at), whole(inv0_s), NN), at))
+
+    def prepare_mix():
+        @pl.when(core == 0)
+        def _():
+            over(lambda at: keep(other_s, dot3(by_rows(g_s, at), whole(p_s), NN), at))
+
+            def add(at):
+                high, low = by_rows(own_s, at)
+                more = dot3(by_columns(p_s, at), whole(other_s), TN)
+                keep(own_s, high.astype(F32) + (low.astype(F32) + more), at)
+
+            over(add)
+
+        @pl.when(core == 1)
+        def _():
+            over(lambda at: keep(other_s, dot3(by_columns(p_s, at), whole(own_s), TN), at))
 
     def each_slot(own, others, work, send):
         ready = None
@@ -270,7 +286,7 @@
                 yield pl.ds(r * 8, 8), pl.ds(c * LANES, LANES)
 
     def sums(u, s, send):
-        marks = [par_v[s, k] for k in range(GROUP)]
+        marks = [jnp.broadcast_to(par_v[s, k], (8, LANES)) for k in range(GROUP)]
 
         def work(j, into):
             chosen = [mark == peers[1 - s][j] for mark in marks]
@@ -283,7 +299,7 @@
         each_slot(recv2, send2, work, send)
 
     def picks(u, s, send):
-        marks = [par_v[s, k] for k in range(GROUP)]
+        marks = [jnp.broadcast_to(par_v[s, k], (8, LANES)) for k in range(GROUP)]
 
         def work(k, into):
             chosen = [marks[k] == peers[1 - s][j] for j in range(GROUP)]
@@ -318,30 +334,16 @@
         loads[0, u] = load
         swap(u).start()
 
-        @pl.when(core == 0)
-        def _():
-            kept[0, u] = thin_dot3(load, whole(own_s), NN)
-            kept[1, u] = thin_dot3(load, whole(p_s), NT)
+        kept[u] = thin_dot3(load, whole(own_s), NN)
 
     def solve(u):
         swap(u).wait_recv()
 
-        def give(solution):
-            for s in range(2):
-                recv3[u, s, 0] = solution[s * part : (s + 1) * part]
-            for c in range(width):
-                front_out[pl.ds(u * unit * width + c, unit, stride=width), :] = solution[:, c * LANES : (c + 1) * LANES]
-
-        @pl.when(core == 0)
-        def _():
-            later = thin_dot3(loads[1, u] - kept[1, u], whole(g_s), NN)
-            give(kept[0, u] - thin_dot3(later, whole(p_s), NN))
-
-        @pl.when(core == 1)
-        def _():
-            pending = loads[0, u] - thin_dot3(loads[1, u], whole(p_s), NT)
-            give(thin_dot3(pending, whole(g_s), NN))
-
+        solution = kept[u] - thin_dot3(loads[1, u], whole(other_s), NN)
+        for s in range(2):
+            recv3[u, s, 0] = solution[s * part : (s + 1) * part]
+        for c in range(width):
+            front_out[pl.ds(u * unit * width + c, unit, stride=width), :] = solution[:, c * LANES : (c + 1) * LANES]
         for s in range(2):
             gather_start(u, s, 1 - s, recv3, out3, in3)
 
@@ -356,7 +358,7 @@
         for c in range(2):
             leaf_out[pl.ds(u * unit * 2 + c, unit, stride=2), :] = result[:, c * LANES : (c + 1) * LANES]
 
-    plan = [(0.0, prepare_last), (0.5, prepare_own), (3.5, prepare_other), (5.9, prepare_product)]
+    plan = [(0.5, prepare_own), (3.5, prepare_other), (5.9, prepare_product), (8.4, prepare_mix), (15.0, prepare_last)]
     stages = (
         (4.7, 1.2, sum_updates), (9.5, 1.2, swap_load), (10.7, 1.2, solve), (15.8, 1.2, pick_panels), (20.8, 1.2, finish),
     )
@@ -420,11 +422,12 @@
             pltpu.VMEM((crows, snode), F32),
             pltpu.VMEM((1, crows), jnp.int32),
             square, square, square,
-            pltpu.VMEM((2, GROUP, 8, LANES), jnp.int32),
+            pltpu.VMEM((2, GROUP, 1, LANES), jnp.int32),
             slots, slots, slots, slots, slots, slots,
-            halves, halves,
+            halves,
+            pltpu.VMEM((UNITS, 2 * part, panel), F32),
             pltpu.VMEM((count, snode), F32),
-            pair, pair, pair, pair, pair, pair,
+            pair, pair, pair, pair, pair, pair, pair,
             pltpu.VMEM((2, panel, snode), BF16),
             pltpu.VMEM((panel, crows), BF16),
             dma((8,)), dma, dma((2, GROUP)), dma((3,)), dma((3,)), dma((UNITS,)), dma((UNITS,)),

time: 40.6 us -> 39.9 us (0.983)
  the two profiles are of different devices: /device:TPU:1 before, /device:TPU:0 now
where the time goes in v5:
time: 39.9 us; the launch traced here: 39.2 us
  Pallas kernels  37.9 us (95%)
  between operations  1.29 us (3%)
    pallas_call x1, Pallas kernels, on_device(): pl.pallas_call(kernel, out_shape=(pltpu.VMEM((count * snode // LANES, LAN...  37.2 us

profile of v5, /device:TPU:0, one launch (start us, length us, event | category | flops | bytes accessed | tf_op | source)
XLA Modules:
  0.0 39.2 jit_solution(1041736924518236633)
XLA Ops:
  1.3 37.2 %shard_map.95 = (f32[128,128]{1,0:T(8,128)S(1)}, f32[256,128]{1,0:T(8,128)S(1)}) custom-call(f32[128,128]{1,0:T(8,128)} %bitcast.14, f32[256,128]{1,0:T(8,128)} %bitcast.13, f32[256,256]{1,0:T(8,128)} %bitcast.12, f32[384,256]{1,0:T(8,128)} %bitcast.11, f32[512,1024]{1,0:T(8,128)} %bitcast.9, f32[512,512]{1,0:T(8,128)} %bitcast.10, s32[1,384]{1,0:T(1,128)} %bitcast.15, ...), custom_call_target="tpu_custom_call" | custom-call | tf_op jit(solution)/shard_map/pallas_call | solution.py:410
  38.5 0.7 %shard_map.96 = (f32[128,128]{1,0:T(8,128)}, f32[256,128]{1,0:T(8,128)}) custom-call(f32[128,128]{1,0:T(8,128)S(1)} %get-tuple-element.6.leaf_in, f32[256,128]{1,0:T(8,128)S(1)} %get-tuple-element.7.front_in), custom_call_target="tpu_custom_call" | custom-call | tf_op jit(solution)/shard_map/pallas_call | solution.py:453
